TPU v7x, 32 devices: a whole 2x2x4 slice. The times are simulated.
32 devices in a mesh: section: 4 (over z), ctx: 8 (over y, x, core).
Axes of the slice: x: 2, y: 2, z: 4, core: 2. Of those that a mesh axis runs over, the one named last changes fastest.
Arguments:
- queries: bfloat16 [4, 1024, 2048], P('section', 'ctx'), may hold values from -120 to 120
- keys_values: bfloat16 [4, 1024, 256], P('section', 'ctx'), may hold values from -6 to 6
- output: bfloat16 [4, 1024, 2048], P('section', 'ctx'), may hold values from -0.59765625 to 0.59765625
- dout: bfloat16 [4, 1024, 2048], P('section', 'ctx'), may hold values from -1.796875 to 1.796875
- segment_ids: int32 [4, 1024], P('section', 'ctx'), may hold values from 0 to 3, as said below
- span_order: int32 [16], P('ctx'), may hold values from 0 to 15, as said below
Outputs:
- upstream_query_grads: bfloat16 [4, 1024, 2048], P('section', 'ctx')
- upstream_kv_grads: bfloat16 [4, 1024, 256], P('section', 'ctx')
Inputs may be any that keep to these rules, and one draw needn't show every extreme that they name: `span_order`: entries 2j and 2j + 1 are a span c below 8 and its mirror 16 - 1 - c; every span appears once. `segment_ids`: read in sequence position order, each section's document numbers never fall, and all 4 documents are present.
All inputs are finite; a program needn't handle non-finite values.
Results may differ from a plain program's by a relative error of at most 0.012.
Values may be sent and summed in bfloat16 or wider, within the bound.
A program may use at most 64 MiB of HBM per device.

v0:
```python
import math

import jax
import jax.numpy as jnp
from jax import lax
from jax.sharding import PartitionSpec as P

NEG = -1e30


def from_behind(value, axis, steps):
    count = lax.axis_size(axis)
    initial, last = (max(0, -steps), min(count, count - steps))
    return lax.ppermute(value, axis, [(source, source + steps) for source in range(initial, last)])


def arrange_rows(block, span, heads, head):
    return block.reshape(2, span, heads, head).transpose(0, 2, 1, 3).reshape(2, heads * span, head)


def pick_rows(early, pair):
    count = early.shape[0]
    shape = (count,) + pair.shape[1:]
    flags = early.reshape((count,) + (1,) * (pair.ndim - 1))
    chosen = jnp.where(flags, pair[0][None], pair[1][None])
    return jnp.concatenate([jnp.broadcast_to(pair[1][None], shape), chosen], axis=0)


def pick_keys(early, grouped):
    count = early.shape[0]
    flags = early.reshape((count,) + (1,) * (grouped.ndim - 2))
    chosen = jnp.where(flags, grouped[:, 0], grouped[:, 1])
    return jnp.concatenate([grouped[:, 0], chosen], axis=0)


def block_scores(keys, rows, key_pos, key_seg, row_pos, row_seg, scale):
    scores = (
        lax.dot_general(
            keys, rows, (((2,), (2,)), ((0,), (0,))), preferred_element_type=jnp.float32
        )
        * scale
    )
    allowed = (key_pos[:, :, None] <= row_pos[:, None, :]) & (
        key_seg[:, :, None] == row_seg[:, None, :]
    )
    return (scores, allowed)


def block_stats(scores, allowed):
    top = jnp.max(jnp.where(allowed, scores, NEG), axis=1)
    total = jnp.sum(jnp.where(allowed, jnp.exp(scores - top[:, None, :]), 0.0), axis=1)
    return (top, total)


def fold_stats(top, total):
    best = jnp.max(top, axis=0)
    return (best, jnp.sum(total * jnp.exp(top - best[None, :]), axis=0))


def merge_stats(top_a, total_a, top_b, total_b):
    best = jnp.maximum(top_a, top_b)
    return (best, total_a * jnp.exp(top_a - best) + total_b * jnp.exp(top_b - best))


def block_grads(scores, allowed, keys, values, q_sel, d_sel, lse_sel, delta_sel, scale):
    probs = jnp.where(allowed, jnp.exp(scores - lse_sel[:, None, :]), 0.0)
    d_probs = lax.dot_general(
        values, d_sel, (((2,), (2,)), ((0,), (0,))), preferred_element_type=jnp.float32
    )
    d_scores = (probs * (d_probs - delta_sel[:, None, :])).astype(jnp.bfloat16)
    probs_low = probs.astype(jnp.bfloat16)
    row_grad = (
        lax.dot_general(
            d_scores, keys, (((1,), (1,)), ((0,), (0,))), preferred_element_type=jnp.float32
        )
        * scale
    )
    key_grad = (
        lax.dot_general(
            d_scores, q_sel, (((2,), (1,)), ((0,), (0,))), preferred_element_type=jnp.float32
        )
        * scale
    )
    value_grad = lax.dot_general(
        probs_low, d_sel, (((2,), (1,)), ((0,), (0,))), preferred_element_type=jnp.float32
    )
    return (row_grad, jnp.concatenate([key_grad, value_grad], axis=2))


def per_device(queries, keys_values, output, dout, segment_ids, span_order):
    head = keys_values.shape[2] // 2
    tok = queries.shape[1]
    heads = queries.shape[2] // head
    span = tok // 2
    width = heads * span
    scale = head ** (-0.5)
    q_rows = arrange_rows(queries[0], span, heads, head)
    d_rows = arrange_rows(dout[0], span, heads, head)
    o_rows = arrange_rows(output[0], span, heads, head)
    delta = jnp.sum(d_rows.astype(jnp.float32) * o_rows.astype(jnp.float32), axis=2)
    offset = jnp.arange(width, dtype=jnp.int32) % span
    row_pos = span_order[:, None] * span + offset[None, :]
    local_seg = segment_ids[0]
    row_seg = jnp.tile(local_seg.reshape(2, span), (1, heads))
    inside = jnp.tile(jnp.arange(span, dtype=jnp.int32), 2)
    key_pos = jnp.repeat(span_order, span) * span + inside
    local_kv = keys_values[0]
    mine = span_order[0]

    def split_groups(piece):
        kv_piece, pos_piece, seg_piece = piece
        count = kv_piece.shape[0] // tok
        size = math.gcd(count, 4)
        groups = count // size
        return (
            kv_piece.reshape(groups, size, 2, span, 2 * head),
            pos_piece.reshape(groups, size, 2, span),
            seg_piece.reshape(groups, size, 2, span),
        )

    def stats_group(carry, group):
        kv_group, pos_group, seg_group = group
        early = pos_group[:, 0, 0] // span <= mine
        scores, allowed = block_scores(
            pick_keys(early, kv_group[..., :head]),
            pick_rows(early, q_rows),
            pick_keys(early, pos_group),
            pick_keys(early, seg_group),
            pick_rows(early, row_pos),
            pick_rows(early, row_seg),
            scale,
        )
        top, total = block_stats(scores, allowed)
        size = early.shape[0]
        flags = early[:, None]
        early_top, early_total = fold_stats(
            jnp.where(flags, top[size:], NEG), jnp.where(flags, total[size:], 0.0)
        )
        late_top, late_total = fold_stats(
            jnp.concatenate([top[:size], jnp.where(flags, NEG, top[size:])], axis=0),
            jnp.concatenate([total[:size], jnp.where(flags, 0.0, total[size:])], axis=0),
        )
        merged = merge_stats(
            carry[0],
            carry[1],
            jnp.stack([early_top, late_top]),
            jnp.stack([early_total, late_total]),
        )
        return (merged, None)

    diag_keys = local_kv[span:][None]
    diag_pos = key_pos[span:][None]
    diag_seg = local_seg[span:][None]
    diag_scores, diag_allowed = block_scores(
        diag_keys[..., :head], q_rows[1:2], diag_pos, diag_seg, row_pos[1:2], row_seg[1:2], scale
    )
    diag_top, diag_total = block_stats(diag_scores, diag_allowed)
    start_top = jnp.stack([jnp.full((width,), NEG, jnp.float32), diag_top[0]])
    start_total = jnp.stack([jnp.zeros((width,), jnp.float32), diag_total[0]])
    whole_kv, whole_pos, whole_seg = (
        lax.all_gather(local_kv, "ctx", axis=0, tiled=True),
        lax.all_gather(key_pos, "ctx", axis=0, tiled=True),
        lax.all_gather(local_seg, "ctx", axis=0, tiled=True),
    )
    result, unused = lax.scan(
        stats_group, (start_top, start_total), split_groups((whole_kv, whole_pos, whole_seg))
    )
    top, total = result
    lse = top + jnp.log(total)

    def grads_group(dq_acc, group):
        kv_group, pos_group, seg_group = group
        early = pos_group[:, 0, 0] // span <= mine
        keys = pick_keys(early, kv_group[..., :head])
        values = pick_keys(early, kv_group[..., head:])
        q_sel = pick_rows(early, q_rows)
        d_sel = pick_rows(early, d_rows)
        scores, allowed = block_scores(
            keys,
            q_sel,
            pick_keys(early, pos_group),
            pick_keys(early, seg_group),
            pick_rows(early, row_pos),
            pick_rows(early, row_seg),
            scale,
        )
        row_grad, kv_grad = block_grads(
            scores,
            allowed,
            keys,
            values,
            q_sel,
            d_sel,
            pick_rows(early, lse),
            pick_rows(early, delta),
            scale,
        )
        size = early.shape[0]
        flags = early.astype(jnp.float32)
        weight_early = jnp.concatenate([jnp.zeros((size,), jnp.float32), flags])
        weight_late = jnp.concatenate([jnp.ones((size,), jnp.float32), 1.0 - flags])
        dq_new = dq_acc + jnp.stack(
            [
                jnp.einsum("b,brd->rd", weight_early, row_grad),
                jnp.einsum("b,brd->rd", weight_late, row_grad),
            ]
        )
        key_early = kv_grad[:size] + flags[:, None, None] * kv_grad[size:]
        key_late = (1.0 - flags)[:, None, None] * kv_grad[size:]
        return (dq_new, jnp.stack([key_early, key_late], axis=1))

    diag_row, diag_kv = block_grads(
        diag_scores,
        diag_allowed,
        diag_keys[..., :head],
        diag_keys[..., head:],
        q_rows[1:2],
        d_rows[1:2],
        lse[1:2],
        delta[1:2],
        scale,
    )
    dq_start = jnp.stack([jnp.zeros((width, head), jnp.float32), diag_row[0]])
    dq_acc = dq_start
    dq_acc, blocks = lax.scan(grads_group, dq_acc, split_groups((whole_kv, whole_pos, whole_seg)))
    terms = blocks.reshape(-1, 2 * head)
    dq_acc, terms = (dq_acc, terms)
    q_grad = (
        dq_acc.reshape(2, heads, span, head)
        .transpose(0, 2, 1, 3)
        .reshape(tok, heads * head)
        .astype(jnp.bfloat16)
    )
    summed = lax.psum_scatter(
        terms.astype(jnp.bfloat16), "ctx", scatter_dimension=0, tiled=True
    ).astype(jnp.float32)
    own_terms = jnp.concatenate([jnp.zeros((span, 2 * head), jnp.float32), diag_kv[0]], axis=0)
    kv_grad = (summed + own_terms).astype(jnp.bfloat16)
    sent_q, sent_kv = from_behind((q_grad, kv_grad), "section", -1)
    return (sent_q[None], sent_kv[None])


def solution(mesh):
    placed = (
        P("section", "ctx", None),
        P("section", "ctx", None),
        P("section", "ctx", None),
        P("section", "ctx", None),
        P("section", "ctx"),
        P("ctx"),
    )
    return jax.shard_map(
        per_device,
        mesh=mesh,
        in_specs=placed,
        out_specs=(P("section", "ctx", None), P("section", "ctx", None)),
        check_vma=False,
    )
```

profile of v0, /device:TPU:0, one launch (start us, length us, event | category | flops | bytes accessed | tf_op | source)
XLA Modules:
  0.0 130.7 jit_solution(11443921508068744047)
XLA Ops:
  7.2 0.7 broadcast_multiply_fusion
  8.1 0.7 slice_bitcast_fusion.20
  8.8 10.4 %all-gather = s32[1,1024]{1,0:T(1,128)S(1)} all-gather(s32[1,128]{1,0:T(1,128)} %param.14), channel_id=2, replica_groups=mesh['section'=4,'ctx'=8] {'ctx'}, dimensions={1}, use_global_device_ids=true | all-gather | bytes 4608 | tf_op jit(solution)/shard_map/all_gather | solution.py:163
  19.2 1.1 copy.60
  22.0 8.7 %all-gather.2 = s32[8,1,128]{2,1,0:T(1,128)S(1)} all-gather(s32[1,1,128]{2,1,0:T(1,128)S(1)} %reshape.272), channel_id=1, replica_groups=mesh['section'=4,'ctx'=8] {'ctx'}, dimensions={0}, use_global_device_ids=true | all-gather | bytes 4608 | tf_op jit(solution)/shard_map/all_gather | solution.py:162
  31.1 0.6 reduce.35
  31.7 0.6 reduce.33
  32.5 0.6 reduce.34
  33.2 9.0 %all-gather.1 = bf16[1,1024,256]{2,1,0:T(8,128)(2,1)S(1)} all-gather(bf16[1,128,256]{2,1,0:T(8,128)(2,1)S(1)} %copy-done.20), channel_id=3, replica_groups=mesh['section'=4,'ctx'=8] {'ctx'}, dimensions={1}, use_global_device_ids=true | all-gather | bytes 589824 | tf_op jit(solution)/shard_map/all_gather | solution.py:161
  42.7 6.5 %while.28 = (s32[]{:T(128)}, f32[2,1024]{1,0:T(2,128)S(1)}, f32[2,1024]{1,0:T(2,128)S(1)}, s32[2,4,2,64]{3,1,2,0:T(4,128)S(1)}, s32[]{:T(128)S(1)}, /*index=5*/s...) while((s32[]{:T(128)}, f32[2,1024]{1,0:T(2,128)S(1)}, ...), condition=%wide.region_10.11_spmd, body=%wide.region_2.10_spmd.sunk | while | flops 142812800 | bytes 12028125 | solution.py:165
  43.8 0.9 select_reduce_fusion.6
  44.7 0.9 select_reduce_fusion.7
  47.0 0.9 select_reduce_fusion.6
  48.0 0.9 select_reduce_fusion.7
  50.0 0.6 copy-done.2
  51.0 29.0 %while.29 = (s32[]{:T(128)}, f32[2,1024,128]{2,1,0:T(8,128)S(1)}, bf16[2,4,2,64,256]{4,3,1,2,0:T(8,128)(2,1)S(1)}, s32[2,4,2,64]{3,1,2,0:T(4,128)S(1)}, s32[]{:T...) while((s32[]{:T(128)}, f32[2,1024,128]{2,1,0:T(8,128)S(1)}, ...), condition=%wide.region_13.14_spmd, body=%wide.region_12.13_spmd.sunk | while | flops 689751680 | bytes 40401856 | solution.py:225
  51.2 0.6 fusion.142
  52.2 0.6 pad_add_fusion.23
  52.8 0.6 pad_add_fusion.21
  53.4 1.8 %convert_reduce_fusion.2 = (f32[4]{0:T(128)}, f32[4]{0:T(128)}, pred[4,1,1]{2,0,1:T(4,128)(4,1)}) fusion(s32[]{:T(128)} %copy-done.15, s32[4,2,64]{2,0,1:T(4,128)S(1)} %get-tuple-element.725), kind=kLoop, calls=%fused_computation.120.clone.1 | loop fusion | flops 72 | bytes 56 | tf_op jit(solution)/shard_map/while/body/eval_jaxpr/convert_element_type | solution.py:199
  55.2 1.2 reduce.45
  56.5 0.5 copy-done.23
  57.7 0.9 exponential_select_fusion.3
  58.8 0.8 multiply_convert_fusion.2
  60.2 0.5 fusion.149
  61.0 0.8 convolution_multiply_fusion.5
  61.8 1.4 %fusion.147 = f32[1,1024,128]{2,0,1:T(1,128)S(1)} fusion(bf16[8,1024,128]{2,1,0:T(8,128)(2,1)S(1)} %convolution_multiply_fusion.5, bf16[4]{0:T(256)(128)(2,1)S(1)} %copy-done.24), kind=kOutput, calls=%fused_computation.63.clone.1 | convolution fusion | flops 2097152 | bytes 2621448 | tf_op jit(solution)/shard_map/while/body/eval_jaxpr/b,brd->rd/dot_general | solution.py:204
  63.3 1.4 %fusion.146 = f32[1,1024,128]{2,0,1:T(1,128)S(1)} fusion(bf16[8,1024,128]{2,1,0:T(8,128)(2,1)S(1)} %convolution_multiply_fusion.5, bf16[4]{0:T(256)(128)(2,1)S(1)} %broadcast_subtract_fusion.2), kind=kOutput, calls=%fused_computation.61.clone.1 | convolution fusion | flops 2097152 | bytes 2621448 | tf_op jit(solution)/shard_map/while/body/eval_jaxpr/b,brd->rd/dot_general | solution.py:205
  65.6 0.6 fusion.142
  66.6 0.6 pad_add_fusion.23
  67.3 0.6 pad_add_fusion.21
  67.8 1.8 %convert_reduce_fusion.2 = (f32[4]{0:T(128)}, f32[4]{0:T(128)}, pred[4,1,1]{2,0,1:T(4,128)(4,1)}) fusion(s32[]{:T(128)} %copy-done.15, s32[4,2,64]{2,0,1:T(4,128)S(1)} %get-tuple-element.725), kind=kLoop, calls=%fused_computation.120.clone.1 | loop fusion | flops 72 | bytes 56 | tf_op jit(solution)/shard_map/while/body/eval_jaxpr/convert_element_type | solution.py:199
  69.7 1.2 reduce.45
  71.0 0.5 copy-done.23
  72.2 0.9 exponential_select_fusion.3
  73.3 0.8 multiply_convert_fusion.2
  74.6 0.5 fusion.149
  75.5 0.8 convolution_multiply_fusion.5
  76.3 1.4 %fusion.147 = f32[1,1024,128]{2,0,1:T(1,128)S(1)} fusion(bf16[8,1024,128]{2,1,0:T(8,128)(2,1)S(1)} %convolution_multiply_fusion.5, bf16[4]{0:T(256)(128)(2,1)S(1)} %copy-done.24), kind=kOutput, calls=%fused_computation.63.clone.1 | convolution fusion | flops 2097152 | bytes 2621448 | tf_op jit(solution)/shard_map/while/body/eval_jaxpr/b,brd->rd/dot_general | solution.py:204
  77.8 1.4 %fusion.146 = f32[1,1024,128]{2,0,1:T(1,128)S(1)} fusion(bf16[8,1024,128]{2,1,0:T(8,128)(2,1)S(1)} %convolution_multiply_fusion.5, bf16[4]{0:T(256)(128)(2,1)S(1)} %broadcast_subtract_fusion.2), kind=kOutput, calls=%fused_computation.61.clone.1 | convolution fusion | flops 2097152 | bytes 2621448 | tf_op jit(solution)/shard_map/while/body/eval_jaxpr/b,brd->rd/dot_general | solution.py:205
  80.0 0.8 copy.55
  81.4 1.3 collective-permute-start
  83.2 32.1 %reduce-scatter.2.cloned.1.call-done = bf16[128,256]{1,0:T(8,128)(2,1)} async-done(((bf16[1024,256]{1,0:T(8,128)(2,1)}), bf16[128,256]{1,0:T(8,128)(2,1)}) %reduce-scatter.2.cloned.1.call-update) | async-done | bytes 65552 | tf_op jit(solution)/shard_map/reduce_scatter | solution.py:234
  115.4 0.8 add_convert_fusion
  116.2 1.3 collective-permute-start.1
  117.5 4.8 %collective-permute-done.1 = bf16[128,256]{1,0:T(8,128)(2,1)S(1)} collective-permute-done((bf16[128,256]{1,0:T(8,128)(2,1)S(1)}, bf16[128,256]{1,0:T(8,128)(2,1)S(1)}, u32[]{:S(2)}, u32[]{:S(2)}) %collective-permute-start.1) | collective-permute-done | bytes 65568 | tf_op jit(solution)/shard_map/ppermute | solution.py:14
  122.4 0.8 copy.104
  123.2 0.6 copy.105
  (255 shorter events, 13.1 us)
Async XLA Ops:
  7.2 13.3 %copy-start = (bf16[1,128,2048]{2,1,0:T(8,128)(2,1)S(1)}, bf16[1,128,2048]{2,1,0:T(8,128)(2,1)}, u32[]{:S(2)}) copy-start(bf16[1,128,2048]{2,1,0:T(8,128)(2,1)} %param.12) | copy-start | bytes 1572868
  7.2 108.2 %reduce-scatter.2.cloned.1.call-start = ((), (), s32[]{:S(2)}) async-start(), calls=%async_computation.1 | async-start | bytes 589824 | tf_op jit(solution)/shard_map/reduce_scatter | solution.py:234
  8.0 41.4 %copy-start.33 = (s32[64]{0:T(128)}, s32[64]{0:T(128)S(1)}, u32[]{:S(2)}) copy-start(s32[64]{0:T(128)S(1)} %slice_bitcast_fusion.21) | copy-start | bytes 772
  8.8 40.6 %copy-start.31 = (s32[64]{0:T(128)}, s32[64]{0:T(128)S(1)}, u32[]{:S(2)}) copy-start(s32[64]{0:T(128)S(1)} %slice_bitcast_fusion.20) | copy-start | bytes 772
  20.6 1.0 copy-start.1
  20.8 10.3 %copy-start.35 = (s32[1,128]{1,0:T(1,128)S(1)}, s32[1,128]{1,0:T(1,128)}, u32[]{:S(2)}) copy-start(s32[1,128]{1,0:T(1,128)} %param.14) | copy-start | bytes 1540
  20.8 12.4 %copy-start.20 = (bf16[1,128,256]{2,1,0:T(8,128)(2,1)S(1)}, bf16[1,128,256]{2,1,0:T(8,128)(2,1)}, u32[]{:S(2)}) copy-start(bf16[1,128,256]{2,1,0:T(8,128)(2,1)} %param.11) | copy-start | bytes 196612
  21.3 20.9 %copy-start.17 = (f32[2,16,64]{2,1,0:T(8,128)}, f32[2,16,64]{2,1,0:T(8,128)S(1)}, u32[]{:S(2)}) copy-start(f32[2,16,64]{2,1,0:T(8,128)S(1)} %fusion.62) | copy-start | bytes 24580
  21.5 27.9 %copy-start.25 = (s32[1024]{0:T(1024)}, s32[1024]{0:T(1024)S(1)}, u32[]{:S(2)}) copy-start(s32[1024]{0:T(1024)S(1)} %tile.23) | copy-start | bytes 12292
  21.6 27.8 %copy-start.27 = (s32[1,1024]{1,0:T(1,128)}, s32[1,1024]{1,0:T(1,128)S(1)}, u32[]{:S(2)}) copy-start(s32[1,1024]{1,0:T(1,128)S(1)} %slice.348) | copy-start | bytes 12292
  21.8 20.9 %copy-start.14 = (s32[2]{0:T(128)S(1)}, s32[2]{0:T(128)}, u32[]{:S(2)}) copy-start(s32[2]{0:T(128)} %param.15) | copy-start | bytes 28
  42.5 6.9 %copy-start.10 = (f32[64,1024]{1,0:T(8,128)}, f32[64,1024]{1,0:T(8,128)S(1)}, u32[]{:S(2)}) copy-start(f32[64,1024]{1,0:T(8,128)S(1)} %get-tuple-element.505) | copy-start | bytes 786436
  42.7 6.6 %slice-start = ((f32[2,16,64]{2,1,0:T(8,128)}), f32[1,16,64]{2,1,0:T(8,128)S(1)}, s32[]{:S(2)}) async-start(f32[2,16,64]{2,1,0:T(8,128)} %copy-done.17), calls=%async_computation.2 | async-start | bytes 16384 | tf_op jit(solution)/shard_map/slice | solution.py:220
  49.2 1.7 %copy-start.29 = (f32[1,1024]{1,0:T(1,128)}, f32[1,1024]{1,0:T(1,128)S(1)}, u32[]{:S(2)}) copy-start(f32[1,1024]{1,0:T(1,128)S(1)} %slice.350) | copy-start | bytes 12292
  49.3 0.7 copy-start.12
  51.0 1.1 copy-start.4
  51.0 1.0 copy-start.6
  51.0 1.0 copy-start.8
  51.0 1.0 copy-start.15
  57.0 0.7 copy-start.18
  57.0 0.7 copy-start.19
  60.2 0.7 copy-start.22
  60.9 0.9 copy-start.24
  64.8 0.7 copy-start.5
  64.8 0.7 copy-start.7
  64.8 0.7 copy-start.9
  64.8 0.7 copy-start.16
  65.5 1.0 copy-start.4
  65.5 1.0 copy-start.6
  65.5 1.0 copy-start.8
  65.5 1.0 copy-start.15
  71.5 0.7 copy-start.18
  71.5 0.7 copy-start.19
  75.4 0.9 copy-start.24
  79.2 0.7 copy-start.5
  79.2 0.7 copy-start.7
  79.2 0.7 copy-start.9
  79.3 0.7 copy-start.16
  80.8 2.0 %copy-start.11 = (f32[64,1024]{1,0:T(8,128)S(1)}, f32[64,1024]{1,0:T(8,128)}, u32[]{:S(2)}) copy-start(f32[64,1024]{1,0:T(8,128)} %copy-done.10) | copy-start | bytes 786436
  80.8 2.0 %copy-start.13 = (bf16[1,16,64,128]{3,2,1,0:T(8,128)(2,1)S(1)}, bf16[1,16,64,128]{3,2,1,0:T(8,128)(2,1)}, u32[]{:S(2)}) copy-start(bf16[1,16,64,128]{3,2,1,0:T(8,128)(2,1)} %copy-done.12) | copy-start | bytes 786436
  80.8 2.0 %copy-start.26 = (s32[1024]{0:T(1024)S(1)}, s32[1024]{0:T(1024)}, u32[]{:S(2)}) copy-start(s32[1024]{0:T(1024)} %copy-done.25) | copy-start | bytes 12292
  80.8 2.0 %copy-start.28 = (s32[1,1024]{1,0:T(1,128)S(1)}, s32[1,1024]{1,0:T(1,128)}, u32[]{:S(2)}) copy-start(s32[1,1024]{1,0:T(1,128)} %copy-done.27) | copy-start | bytes 12292
  80.8 2.0 %copy-start.30 = (f32[1,1024]{1,0:T(1,128)S(1)}, f32[1,1024]{1,0:T(1,128)}, u32[]{:S(2)}) copy-start(f32[1,1024]{1,0:T(1,128)} %copy-done.29) | copy-start | bytes 12292
  80.8 2.0 %copy-start.32 = (s32[64]{0:T(128)S(1)}, s32[64]{0:T(128)}, u32[]{:S(2)}) copy-start(s32[64]{0:T(128)} %copy-done.31) | copy-start | bytes 772
  80.8 2.0 %copy-start.34 = (s32[64]{0:T(128)S(1)}, s32[64]{0:T(128)}, u32[]{:S(2)}) copy-start(s32[64]{0:T(128)} %copy-done.33) | copy-start | bytes 772
  80.8 2.2 %copy-start.3 = (bf16[64,1024]{1,0:T(8,128)(2,1)S(1)}, bf16[64,1024]{1,0:T(8,128)(2,1)}, u32[]{:S(2)}) copy-start(bf16[64,1024]{1,0:T(8,128)(2,1)} %copy-done.2) | copy-start | bytes 393220
  81.4 36.1 %collective-permute-start = (bf16[128,2048]{1,0:T(8,128)(2,1)S(1)}, bf16[128,2048]{1,0:T(8,128)(2,1)S(1)}, u32[]{:S(2)}, u32[]{:S(2)}) collective-permute-start(bf16[128,2048]{1,0:T(8,128)(2,1)S(1)} %bitcast.312), channel_id=1, source_target_pairs={{8,0},{16,8},{24,16},{9,1},{17,9},{25,17},{10,2},{18,10},{26,18},{... | collective-permute-start | bytes 1572872 | tf_op jit(solution)/shard_map/ppermute | solution.py:14
  116.2 6.2 %collective-permute-start.1 = (bf16[128,256]{1,0:T(8,128)(2,1)S(1)}, bf16[128,256]{1,0:T(8,128)(2,1)S(1)}, u32[]{:S(2)}, u32[]{:S(2)}) collective-permute-start(bf16[128,256]{1,0:T(8,128)(2,1)S(1)} %add_convert_fusion), channel_id=1, source_target_pairs={{8,0},{16,8},{24,16},{9,1},{17,9},{25,17},{10,2},{18,10},{26,18},{... | collective-permute-start | bytes 196616 | tf_op jit(solution)/shard_map/ppermute | solution.py:14
  (6 other events, 3.8 us)
Sparse Core Ops, SparseCore 0:
  81.0 34.3 reduce-scatter.1
where the time goes:
time: 131 us
  waiting for transfers between devices  37 us (28%)
  blocking collectives  28 us (21%)
  other arithmetic  19.6 us (15%)
  matrix products  16 us (12%)
  between operations  14.5 us (11%)
  local copies, waits for them, and re-layouts  12 us (9%)
  starting transfers between devices  2.62 us (2%)
    reduce_scatter x1, waiting for transfers between devices, per_device(): lax.psum_scatter(terms.astype(jnp.bfloat16), 'ctx', scatter_dimension=0,...  32.1 us
    all_gather x1, blocking collectives, per_device(): lax.all_gather(local_seg, 'ctx', axis=0, tiled=True)  10.4 us
    all_gather x1, blocking collectives, per_device(): lax.all_gather(local_kv, 'ctx', axis=0, tiled=True)  8.99 us
    all_gather x1, blocking collectives, per_device(): lax.all_gather(key_pos, 'ctx', axis=0, tiled=True)  8.66 us
    convert_element_type x4, other arithmetic, grads_group(): flags = early.astype(jnp.float32)  4.91 us
    ppermute x2, waiting for transfers between devices, from_behind(): lax.ppermute(value, axis, [(source, source + steps) for source in range(i...  4.85 us
    unnamed x51, local copies, waits for them, and re-layouts  4.27 us
    dot_general x5, matrix products, block_scores(): lax.dot_general(keys, rows, (((2,), (2,)), ((0,), (0,))), preferred_eleme...  3.89 us
  transfers between devices with their start and end apart: 3, of which 2 were waited for; matrix products, arithmetic and copies ran while one was open for 1% of the time, Pallas kernels for 0%

commit v1 on v0

v1 whole, which is shorter than its diff:
```python
import functools

import jax
import jax.numpy as jnp
from jax import lax
from jax.experimental import pallas as pl
from jax.experimental.pallas import tpu as pltpu
from jax.sharding import PartitionSpec as P

MESH = pl.DeviceIdType.MESH
NEG = -1e30
DOT = functools.partial(lax.dot_general, preferred_element_type=jnp.float32)
NT = (((1,), (1,)), ((), ()))
NN = (((1,), (0,)), ((), ()))


def kernel(
    sections, n, head, pairs, width,
    q_in, kv_in, o_in, d_in, seg_in, order_in,
    dq_out, dkv_out,
    q_s, o_s, d_s, kv_s, meta_own, meta_s, kt_s, bias_s, sc_s, p_s, ds_s, dk_s, dv_s, dq_st, rs_st, rs_in, kv_st,
    in_sem, own_sem, ag_send, ag_recv, rs_send, rs_recv, dq_send, dq_recv, kvo_send, kvo_recv,
):
    section = lax.axis_index("section")
    me = lax.axis_index("ctx")
    tok = kv_in.shape[1]
    span = tok // 2
    cols = 2 * head
    scale = head ** (-0.5)
    chunk = tok

    def loop(count, body):
        lax.fori_loop(0, count, lambda i, c: (body(i), c)[1], 0)

    def peer(i):
        return lax.rem(me + i + 1, n)

    def in_copies(g):
        at = pl.ds(pl.multiple_of(g * cols, cols), cols)
        return [
            pltpu.make_async_copy(src.at[0, :, at], dst.at[g], in_sem.at[k, g])
            for k, (src, dst) in enumerate(((q_in, q_s), (d_in, d_s), (o_in, o_s)))
        ]

    own_kv = pltpu.make_async_copy(kv_in.at[0], kv_s.at[me], own_sem)
    own_kv.start()

    barrier = pltpu.get_barrier_semaphore()

    def greet(i):
        pl.semaphore_signal(barrier, inc=1, device_id={"ctx": peer(i)}, device_id_type=MESH)

    loop(n - 1, greet)

    @pl.when(section > 0)
    def _():
        pl.semaphore_signal(barrier, inc=1, device_id={"section": section - 1}, device_id_type=MESH)

    @pl.when(section < sections - 1)
    def _():
        pl.semaphore_signal(barrier, inc=1, device_id={"section": section + 1}, device_id_type=MESH)

    loop(pairs, lambda g: [c.start() for c in in_copies(g)][0])

    lane = lax.broadcasted_iota(jnp.int32, (1, tok), 1)
    pos_row = jnp.where(lane < span, order_in[0] * span + lane, order_in[1] * span + lane - span)
    seg_row = seg_in[...]
    meta = jnp.concatenate([pos_row, seg_row, jnp.zeros((6, tok), jnp.int32)], axis=0)
    meta_own[...] = meta

    ends = (section == 0).astype(jnp.int32) + (section == sections - 1).astype(jnp.int32)
    pl.semaphore_wait(barrier, n + 1 - ends)

    def ag_copies(to, slot):
        return [
            pltpu.make_async_remote_copy(
                src, dst.at[slot], ag_send.at[k, to], ag_recv.at[k, slot],
                device_id={"ctx": to}, device_id_type=MESH,
            )
            for k, (src, dst) in enumerate(((kv_in.at[0], kv_s), (meta_own, meta_s)))
        ]

    loop(n - 1, lambda i: [c.start() for c in ag_copies(peer(i), me)][0])

    meta_s[me] = meta
    dk_s[...] = jnp.zeros_like(dk_s)
    dv_s[...] = jnp.zeros_like(dv_s)
    own_kv.wait()

    def arrive(i):
        for c in ag_copies(peer(i), peer(i)):
            c.wait_recv()

    loop(n - 1, arrive)

    pos_rows = pos_row.astype(jnp.float32)
    seg_rows = seg_row.astype(jnp.float32)

    def prepare(j):
        info = meta_s[j].astype(jnp.float32).T
        ok = (info[:, 0:1] <= pos_rows) & (info[:, 1:2] == seg_rows)
        bias_s[j] = jnp.where(ok, 0.0, NEG)
        kt_s[j] = kv_s[j, :, :head].astype(jnp.float32).T.astype(jnp.bfloat16)

    loop(n, prepare)
    loop(pairs, lambda g: [c.wait() for c in in_copies(g)][0])

    def dq_copy(g):
        at = pl.ds(pl.multiple_of(g * cols, cols), cols)
        return pltpu.make_async_remote_copy(
            dq_st.at[g], dq_out.at[0, :, at], dq_send.at[g], dq_recv.at[g],
            device_id={"section": section - 1}, device_id_type=MESH,
        )

    unroll = n <= 8

    def each(init, body):
        return lax.fori_loop(0, n, body, init, unroll=unroll)

    def pair(g):
        q2, d2, o2 = q_s[g], d_s[g], o_s[g]
        q2 = jnp.concatenate([q2[:, :head], q2[:, head:]], axis=0)
        d2 = jnp.concatenate([d2[:, :head], d2[:, head:]], axis=0)
        o2 = jnp.concatenate([o2[:, :head], o2[:, head:]], axis=0)
        delta = jnp.sum((d2.astype(jnp.float32) * o2.astype(jnp.float32)).T, axis=0, keepdims=True)

        def score(j, top):
            bias = bias_s[j]
            s = DOT(kv_s[j, :, :head], q2, NT) * scale + jnp.concatenate([bias, bias], axis=1)
            sc_s[j] = s
            return jnp.maximum(top, jnp.max(s, axis=0, keepdims=True))

        top = each(jnp.full((1, 2 * tok), NEG, jnp.float32), score)

        def expo(j, total):
            e = jnp.exp(sc_s[j] - top)
            sc_s[j] = e
            return total + jnp.sum(e, axis=0, keepdims=True)

        total = each(jnp.zeros((1, 2 * tok), jnp.float32), expo)
        inv = 1.0 / total

        def grads(j, acc):
            p = sc_s[j] * inv
            dp = DOT(kv_s[j, :, head:], d2, NT)
            ds = (p * (dp - delta)).astype(jnp.bfloat16)
            dk_s[j] += DOT(ds, q2, NN)
            dv_s[j] += DOT(p.astype(jnp.bfloat16), d2, NN)
            return acc + DOT(kt_s[j], ds, NN)

        dqt = each(jnp.zeros((head, 2 * tok), jnp.float32), grads)
        dq = (dqt * scale).T
        dq_st[g] = jnp.concatenate([dq[:tok], dq[tok:]], axis=1).astype(jnp.bfloat16)

        @pl.when(section > 0)
        def _():
            dq_copy(g).start()

    loop(pairs, pair)

    def rs_copy(to, slot):
        return pltpu.make_async_remote_copy(
            rs_st.at[to], rs_in.at[slot], rs_send.at[to], rs_recv.at[slot],
            device_id={"ctx": to}, device_id_type=MESH,
        )

    def scatter(i):
        to = peer(i)
        rs_st[to] = jnp.concatenate([dk_s[to] * scale, dv_s[to]], axis=1).astype(jnp.bfloat16)
        rs_copy(to, me).start()

    loop(n - 1, scatter)

    def gather(i, acc):
        frm = peer(i)
        rs_copy(frm, frm).wait_recv()
        return acc + rs_in[frm].astype(jnp.float32)

    own = jnp.concatenate([dk_s[me] * scale, dv_s[me]], axis=1)
    kv_st[...] = lax.fori_loop(0, n - 1, gather, own).astype(jnp.bfloat16)
    kvo = pltpu.make_async_remote_copy(
        kv_st, dkv_out.at[0], kvo_send, kvo_recv,
        device_id={"section": section - 1}, device_id_type=MESH,
    )

    @pl.when(section > 0)
    def _():
        kvo.start()

    def drain(i):
        for c in ag_copies(peer(i), me):
            c.wait_send()
        rs_copy(peer(i), me).wait_send()

    loop(n - 1, drain)

    @pl.when(section > 0)
    def _():
        loop(pairs, lambda g: dq_copy(g).wait_send())
        kvo.wait_send()

    @pl.when(section < sections - 1)
    def _():
        loop(pairs, lambda g: dq_copy(g).wait_recv())
        kvo.wait_recv()


def per_device(sections, n, queries, keys_values, output, dout, segment_ids, span_order):
    head = keys_values.shape[2] // 2
    tok, width = queries.shape[1:]
    pairs = width // (2 * head)
    cols = 2 * head
    any_spec = pl.BlockSpec(memory_space=pl.ANY)
    f32, bf16, i32 = jnp.float32, jnp.bfloat16, jnp.int32
    dma = pltpu.SemaphoreType.DMA
    dq, dkv = pl.pallas_call(
        functools.partial(kernel, sections, n, head, pairs, width),
        out_shape=(
            jax.ShapeDtypeStruct((1, tok, width), bf16),
            jax.ShapeDtypeStruct((1, tok, cols), bf16),
        ),
        in_specs=[any_spec] * 4
        + [pl.BlockSpec(memory_space=pltpu.VMEM), pl.BlockSpec(memory_space=pltpu.SMEM)],
        out_specs=(any_spec, any_spec),
        scratch_shapes=[
            pltpu.VMEM((pairs, tok, cols), bf16),
            pltpu.VMEM((pairs, tok, cols), bf16),
            pltpu.VMEM((pairs, tok, cols), bf16),
            pltpu.VMEM((n, tok, cols), bf16),
            pltpu.VMEM((8, tok), i32),
            pltpu.VMEM((n, 8, tok), i32),
            pltpu.VMEM((n, head, tok), bf16),
            pltpu.VMEM((n, tok, tok), f32),
            pltpu.VMEM((n, tok, 2 * tok), f32),
            pltpu.VMEM((8, 128), f32),
            pltpu.VMEM((8, 128), f32),
            pltpu.VMEM((n, tok, head), f32),
            pltpu.VMEM((n, tok, head), f32),
            pltpu.VMEM((pairs, tok, cols), bf16),
            pltpu.VMEM((n, tok, cols), bf16),
            pltpu.VMEM((n, tok, cols), bf16),
            pltpu.VMEM((tok, cols), bf16),
            dma((3, pairs)),
            dma,
            dma((2, n)),
            dma((2, n)),
            dma((n,)),
            dma((n,)),
            dma((pairs,)),
            dma((pairs,)),
            dma,
            dma,
        ],
        compiler_params=pltpu.CompilerParams(
            collective_id=0, has_side_effects=True, vmem_limit_bytes=48 << 20
        ),
    )(queries, keys_values, output, dout, segment_ids, span_order)
    last = lax.axis_index("section") == sections - 1
    return (
        jnp.where(last, jnp.zeros_like(dq), dq),
        jnp.where(last, jnp.zeros_like(dkv), dkv),
    )


def solution(mesh):
    rows = P("section", "ctx", None)
    return jax.shard_map(
        functools.partial(per_device, mesh.shape["section"], mesh.shape["ctx"]),
        mesh=mesh,
        in_specs=(rows, rows, rows, rows, P("section", "ctx"), P("ctx")),
        out_specs=(rows, rows),
        check_vma=False,
    )
```

time: 131 us -> 47.5 us (0.36)
  Pallas kernels: 0 us -> 40.4 us
  waiting for transfers between devices: 37 us -> 0 us
  blocking collectives: 28 us -> 0 us
  other arithmetic: 19.6 us -> 1.47 us
  matrix products: 16 us -> 0 us
  between operations: 14.5 us -> 0.67 us
  local copies, waits for them, and re-layouts: 12 us -> 4.62 us
  starting transfers between devices: 2.62 us -> 0 us
    pallas_call x0 -> x1, Pallas kernels: none -> 40.4 us  [per_device(): pl.pallas_call(functools.partial(kernel, sections, n, head, pairs, width)...]
    reduce_scatter x1 -> x0, waiting for transfers between devices: 32.1 us -> none  [per_device(): lax.psum_scatter(terms.astype(jnp.bfloat16), 'ctx', scatter_dimension=0,...]
    all_gather x3 -> x0, blocking collectives: 28 us -> none  [the longest x1 10.4 us: per_device(): lax.all_gather(local_seg, 'ctx', axis=0, tiled=True)]
    dot_general x21 -> x0, matrix products: 16 us -> none  [the longest x5 3.89 us: block_scores(): lax.dot_general(keys, rows, (((2,), (2,)), ((0,), (0,))), preferred_eleme...]
    convert_element_type x6 -> x0, other arithmetic: 5.83 us -> none  [the longest x4 4.91 us: grads_group(): flags = early.astype(jnp.float32)]
    ppermute x2 -> x0, waiting for transfers between devices: 4.85 us -> none  [from_behind(): lax.ppermute(value, axis, [(source, source + steps) for source in range(i...]
    le x6 -> x0, other arithmetic: 2.82 us -> none  [the longest x2 2.41 us: grads_group(): early = pos_group[:, 0, 0] // span <= mine]
    reduce_sum x8 -> x0, other arithmetic: 2.71 us -> none  [the longest x3 1.97 us: block_stats(): jnp.sum(jnp.where(allowed, jnp.exp(scores - top[:, None, :]), 0.0), axis=1)]
  transfers between devices with their start and end apart: 3 -> 0, of which waited for: 2 -> 0; matrix products, arithmetic and copies ran while one was open for 1% -> 0% of each run, Pallas kernels for 0% -> 0%
where the time goes in v1:
time: 47.5 us; the launch traced here: 47.2 us
  Pallas kernels  40.4 us (85%)
  local copies, waits for them, and re-layouts  4.62 us (10%)
  other arithmetic  1.47 us (3%)
  between operations  0.67 us (1%)
    pallas_call x1, Pallas kernels, per_device(): pl.pallas_call(functools.partial(kernel, sections, n, head, pairs, width)...  40.4 us
    unnamed x12, local copies, waits for them, and re-layouts  4.62 us

profile of v1, /device:TPU:0, one launch (start us, length us, event | category | flops | bytes accessed | tf_op | source)
XLA Modules:
  0.0 47.2 jit_solution(15326966232843490012)
XLA Ops:
  0.6 0.0 copy-start.4
  0.6 0.0 copy-start.5
  0.7 0.6 %copy-done.4 = s32[1,128]{1,0:T(1,128)S(1)} copy-done((s32[1,128]{1,0:T(1,128)S(1)}, s32[1,128]{1,0:T(1,128)}, u32[]{:S(2)}) %copy-start.4) | copy-done | bytes 536
  1.3 0.0 copy-done.5
  1.3 0.0 copy-start
  1.3 1.0 %copy-done = bf16[1,128,2048]{2,1,0:T(8,128)(2,1)S(1)} copy-done((bf16[1,128,2048]{2,1,0:T(8,128)(2,1)S(1)}, bf16[1,128,2048]{2,1,0:T(8,128)(2,1)}, u32[]{:S(2)}) %copy-start) | copy-done | bytes 524312
  2.4 0.0 copy-start.1
  2.4 1.0 %copy-done.1 = bf16[1,128,2048]{2,1,0:T(8,128)(2,1)S(1)} copy-done((bf16[1,128,2048]{2,1,0:T(8,128)(2,1)S(1)}, bf16[1,128,2048]{2,1,0:T(8,128)(2,1)}, u32[]{:S(2)}) %copy-start.1) | copy-done | bytes 524312
  3.4 0.0 copy-start.2
  3.4 1.0 %copy-done.2 = bf16[1,128,2048]{2,1,0:T(8,128)(2,1)S(1)} copy-done((bf16[1,128,2048]{2,1,0:T(8,128)(2,1)S(1)}, bf16[1,128,2048]{2,1,0:T(8,128)(2,1)}, u32[]{:S(2)}) %copy-start.2) | copy-done | bytes 524312
  4.4 0.0 copy-start.3
  4.4 0.8 %copy-done.3 = bf16[1,128,256]{2,1,0:T(8,128)(2,1)S(1)} copy-done((bf16[1,128,256]{2,1,0:T(8,128)(2,1)S(1)}, bf16[1,128,256]{2,1,0:T(8,128)(2,1)}, u32[]{:S(2)}) %copy-start.3) | copy-done | bytes 65560
  5.3 40.4 %shard_map.77 = (bf16[1,128,2048]{2,1,0:T(8,128)(2,1)S(1)}, bf16[1,128,256]{2,1,0:T(8,128)(2,1)S(1)}) custom-call(bf16[1,128,2048]{2,1,0:T(8,128)(2,1)S(1)} %copy-done, bf16[1,128,256]{2,1,0:T(8,128)(2,1)S(1)} %copy-done.3, bf16[1,128,2048]{2,1,0:T(8,128)(2,1)S(1)} %copy-done.1, bf16[1,128,2048]{2,1,0:T(8,128)(2,1)S(1)} %copy-done.2, ...), custom_call_target="tpu_custom_call" | custom-call | tf_op jit(solution)/shard_map/pallas_call | solution.py:216
  45.7 0.8 %broadcast_select_fusion = bf16[1,128,2048]{2,1,0:T(8,128)(2,1)} fusion(bf16[1,128,2048]{2,1,0:T(8,128)(2,1)S(1)} %get-tuple-element.4, pred[]{:T(512)S(6)} %eq.3), kind=kLoop, calls=%fused_computation | loop fusion | flops 262144 | bytes 1048577 | tf_op jit(solution)/shard_map/jit(_where)/select_n | solution.py:260
  46.5 0.6 %broadcast_select_fusion.1 = bf16[1,128,256]{2,1,0:T(8,128)(2,1)} fusion(bf16[1,128,256]{2,1,0:T(8,128)(2,1)S(1)} %get-tuple-element.5, pred[]{:T(512)S(6)} %eq.3), kind=kLoop, calls=%fused_computation.1 | loop fusion | flops 32768 | bytes 131073 | tf_op jit(solution)/shard_map/jit(_where)/select_n | solution.py:261
Async XLA Ops:
  0.6 0.7 %copy-start.4 = (s32[1,128]{1,0:T(1,128)S(1)}, s32[1,128]{1,0:T(1,128)}, u32[]{:S(2)}) copy-start(s32[1,128]{1,0:T(1,128)} %seg_in.1) | copy-start | bytes 1540
  0.6 0.7 %copy-start.5 = (s32[2]{0:T(128)S(1)}, s32[2]{0:T(128)}, u32[]{:S(2)}) copy-start(s32[2]{0:T(128)} %order_in.1) | copy-start | bytes 28
  1.3 1.0 %copy-start = (bf16[1,128,2048]{2,1,0:T(8,128)(2,1)S(1)}, bf16[1,128,2048]{2,1,0:T(8,128)(2,1)}, u32[]{:S(2)}) copy-start(bf16[1,128,2048]{2,1,0:T(8,128)(2,1)} %q_in.1) | copy-start | bytes 1572868
  2.4 1.0 %copy-start.1 = (bf16[1,128,2048]{2,1,0:T(8,128)(2,1)S(1)}, bf16[1,128,2048]{2,1,0:T(8,128)(2,1)}, u32[]{:S(2)}) copy-start(bf16[1,128,2048]{2,1,0:T(8,128)(2,1)} %o_in.1) | copy-start | bytes 1572868
  3.4 1.0 %copy-start.2 = (bf16[1,128,2048]{2,1,0:T(8,128)(2,1)S(1)}, bf16[1,128,2048]{2,1,0:T(8,128)(2,1)}, u32[]{:S(2)}) copy-start(bf16[1,128,2048]{2,1,0:T(8,128)(2,1)} %d_in.1) | copy-start | bytes 1572868
  4.4 0.8 %copy-start.3 = (bf16[1,128,256]{2,1,0:T(8,128)(2,1)S(1)}, bf16[1,128,256]{2,1,0:T(8,128)(2,1)}, u32[]{:S(2)}) copy-start(bf16[1,128,256]{2,1,0:T(8,128)(2,1)} %kv_in.1) | copy-start | bytes 196612

commit v2 on v1

v2 whole, which is shorter than its diff:
```python
import functools

import jax
import jax.numpy as jnp
from jax import lax
from jax.experimental import pallas as pl
from jax.experimental.pallas import tpu as pltpu
from jax.sharding import PartitionSpec as P

MESH = pl.DeviceIdType.MESH
NEG = -1e30
DOT = functools.partial(lax.dot_general, preferred_element_type=jnp.float32)
NT = (((1,), (1,)), ((), ()))
NN = (((1,), (0,)), ((), ()))


def kernel(
    sections, n, head, heads,
    q_in, kv_in, o_in, d_in, seg_in, order_in,
    dq_out, dkv_out,
    q_s, o_s, d_s, kv_s, seg_s, meta_own, meta_s, flag_v, flag_m, k_a, k_b, kt_a, kt_b, bias_a, bias_b,
    sc_a, sc_b, ds_a, ds_be, ds_bl, dka_s, dva_s, dkb_s, dvb_s, dq_st, rs_st, rs_in, kv_st,
    in_sem, own_sem, seg_sem, flag_sem, ag_send, ag_recv, rs_send, rs_recv, dq_send, dq_recv, kvo_send, kvo_recv,
):
    section = lax.axis_index("section")
    me = lax.axis_index("ctx")
    tok = kv_in.shape[1]
    span = tok // 2
    cols = 2 * head
    scale = head ** (-0.5)

    def loop(count, body):
        lax.fori_loop(0, count, lambda i, c: (body(i), c)[1], 0)

    def peer(i):
        return lax.rem(me + i + 1, n)

    quad = 4
    quads = heads // quad
    wide = quad * span

    def in_copies(i):
        g, half, h = i // (2 * quad), lax.rem(i // quad, 2), lax.rem(i, quad)
        at = pl.ds(pl.multiple_of((g * quad + h) * head, head), head)
        rows = pl.ds(pl.multiple_of(half * span, span), span)
        to = pl.ds(pl.multiple_of(h * span, span), span)
        return [
            pltpu.make_async_copy(src.at[0, rows, at], dst.at[g, half, to], in_sem.at[k, i])
            for k, (src, dst) in enumerate(((q_in, q_s), (d_in, d_s), (o_in, o_s)))
        ]

    own_kv = pltpu.make_async_copy(kv_in.at[0], kv_s.at[me], own_sem)
    own_kv.start()
    own_seg = pltpu.make_async_copy(seg_in, seg_s, seg_sem)
    own_seg.start()

    barrier = pltpu.get_barrier_semaphore()

    def greet(i):
        pl.semaphore_signal(barrier, inc=1, device_id={"ctx": peer(i)}, device_id_type=MESH)

    loop(n - 1, greet)

    @pl.when(section > 0)
    def _():
        pl.semaphore_signal(barrier, inc=1, device_id={"section": section - 1}, device_id_type=MESH)

    @pl.when(section < sections - 1)
    def _():
        pl.semaphore_signal(barrier, inc=1, device_id={"section": section + 1}, device_id_type=MESH)

    loop(2 * heads, lambda g: [c.start() for c in in_copies(g)][0])

    lane = lax.broadcasted_iota(jnp.int32, (1, tok), 1)
    pos_row = jnp.where(lane < span, order_in[0] * span + lane, order_in[1] * span + lane - span)
    own_seg.wait()
    seg_row = seg_s[...]
    meta = jnp.concatenate([pos_row, seg_row, jnp.full((6, tok), order_in[0], jnp.int32)], axis=0)
    meta_own[...] = meta

    ends = (section == 0).astype(jnp.int32) + (section == sections - 1).astype(jnp.int32)
    pl.semaphore_wait(barrier, n + 1 - ends)

    def ag_copies(to, slot):
        return [
            pltpu.make_async_remote_copy(
                src, dst.at[slot], ag_send.at[k, to], ag_recv.at[k, slot],
                device_id={"ctx": to}, device_id_type=MESH,
            )
            for k, (src, dst) in enumerate(((kv_in.at[0], kv_s), (meta_own, meta_s)))
        ]

    loop(n - 1, lambda i: [c.start() for c in ag_copies(peer(i), me)][0])

    meta_s[me] = meta
    for acc in (dka_s, dva_s, dkb_s, dvb_s):
        acc[...] = jnp.zeros_like(acc)
    ds_a[(n + 1) * span :] = jnp.zeros((span, wide), jnp.bfloat16)
    kt_a[:, n * span :] = jnp.zeros((head, 2 * span), jnp.bfloat16)

    inside = jnp.where(lane < span, lane, lane - span)
    pos_e = (order_in[0] * span + inside).astype(jnp.float32)
    pos_l = (order_in[1] * span + inside).astype(jnp.float32)
    seg_f = seg_row.astype(jnp.float32)
    seg_r = pltpu.roll(seg_f, span, 1)
    seg_e = jnp.where(lane < span, seg_f, seg_r)
    seg_l = jnp.where(lane < span, seg_r, seg_f)

    def bias_of(key, pos, seg):
        ok = (key[:, 0:1] <= pos) & (key[:, 1:2] == seg)
        return jnp.where(ok, 0.0, NEG)

    def block(j):
        return pl.ds(pl.multiple_of(j * span, span), span)

    def prepare(j):
        got = meta_s[j]
        info = got.astype(jnp.float32).T
        kv = kv_s[j].astype(jnp.float32)
        flag = got[2:3] <= order_in[0]
        flag_v[pl.ds(j, 1)] = flag.astype(jnp.int32)
        bias_a[block(j)] = bias_of(info[:span], pos_l, seg_l)
        k_a[block(j)] = kv_s[j, :span]
        kind = jnp.where(flag, 1.0, 0.0)
        lanes2 = jnp.concatenate([kind, kind], axis=1)
        kv_b = jnp.where(lanes2 > 0.5, kv[:span], kv[span:])
        k_b[block(j)] = kv_b.astype(jnp.bfloat16)
        info_b = jnp.where(kind[:, :8] > 0.5, info[:span], info[span:])
        bias_b[block(j)] = bias_of(
            info_b, jnp.where(flag, pos_e, pos_l), jnp.where(flag, seg_e, seg_l)
        )

        @pl.when(j == me)
        def _():
            last = pl.ds(n * span, span)
            k_a[last] = kv_s[j, span:]
            bias_a[last] = bias_of(info[span:], pos_l, seg_l)

    own_kv.wait()
    prepare(me)

    def arrive(i):
        for c in ag_copies(peer(i), peer(i)):
            c.wait_recv()
        prepare(peer(i))

    loop(n - 1, arrive)
    flags = pltpu.make_async_copy(flag_v, flag_m, flag_sem)
    flags.start()

    def turn(j):
        at = pl.ds(pl.multiple_of(j * tok, tok), tok)
        rows = pl.ds(pl.multiple_of(j * tok, tok), tok)
        kt_a[:, at] = k_a[rows, :head].astype(jnp.float32).T.astype(jnp.bfloat16)
        kt_b[:, at] = k_b[rows, :head].astype(jnp.float32).T.astype(jnp.bfloat16)

    loop(n // 2, turn)
    kt_a[:, pl.ds(n * span, tok)] = jnp.concatenate(
        [k_a[pl.ds(n * span, span), :head].astype(jnp.float32).T, jnp.zeros((head, span), jnp.float32)],
        axis=1,
    ).astype(jnp.bfloat16)
    loop(2 * heads, lambda g: [c.wait() for c in in_copies(g)][0])
    flags.wait()

    def dq_copy(g):
        at = pl.ds(pl.multiple_of(g * quad * head, quad * head), quad * head)
        return pltpu.make_async_remote_copy(
            dq_st.at[g], dq_out.at[0, :, at], dq_send.at[g], dq_recv.at[g],
            device_id={"section": section - 1}, device_id_type=MESH,
        )

    size = max(d for d in range(1, 17) if (n + 1) % d == 0)
    steps = (n + 1) // size
    size *= span

    def each(count, init, body):
        return lax.fori_loop(0, count, body, init, unroll=count <= 8)

    def part(c):
        return pl.ds(pl.multiple_of(c * size, span), size)

    def twice(x):
        return jnp.concatenate([x, x], axis=1)

    def group(g):
        q_l, d_l = q_s[g, 1], d_s[g, 1]

        def delta_of(half):
            prod = d_s[g, half].astype(jnp.float32) * o_s[g, half].astype(jnp.float32)
            return jnp.sum(prod.T, axis=0, keepdims=True)

        delta_e, delta_l = delta_of(0), delta_of(1)

        def flag_of(j):
            return flag_m[j, 0]

        def choose(f, early, late):
            return jnp.where(f > 0, early, late)

        low = jnp.full((1, wide), NEG, jnp.float32)
        none = jnp.zeros((1, wide), jnp.float32)

        def score_a(c, top):
            s = DOT(k_a[part(c), :head], q_l, NT) * scale + twice(bias_a[part(c)])
            sc_a[part(c)] = s
            return jnp.maximum(top, jnp.max(s, axis=0, keepdims=True))

        def score_b(j, tops):
            f = flag_of(j)
            s = DOT(k_b[block(j), :head], q_s[g, 1 - f], NT) * scale + twice(bias_b[block(j)])
            sc_b[block(j)] = s
            top = jnp.max(s, axis=0, keepdims=True)
            return (
                jnp.maximum(tops[0], choose(f, top, low)),
                jnp.maximum(tops[1], choose(f, low, top)),
            )

        top_e, top_l = each(n, (low, each(steps, low, score_a)), score_b)

        def exp_a(c, total):
            e = jnp.exp(sc_a[part(c)] - top_l)
            sc_a[part(c)] = e
            return total + jnp.sum(e, axis=0, keepdims=True)

        def exp_b(j, totals):
            f = flag_of(j)
            e = jnp.exp(sc_b[block(j)] - choose(f, top_e, top_l))
            sc_b[block(j)] = e
            total = jnp.sum(e, axis=0, keepdims=True)
            return (totals[0] + choose(f, total, none), totals[1] + choose(f, none, total))

        total_e, total_l = each(n, (none, each(steps, none, exp_a)), exp_b)
        inv_e, inv_l = 1.0 / total_e, 1.0 / total_l

        def grads_a(c, unused):
            p = sc_a[part(c)] * inv_l
            dp = DOT(k_a[part(c), head:], d_l, NT)
            ds = (p * (dp - delta_l)).astype(jnp.bfloat16)
            ds_a[part(c)] = ds
            dka_s[part(c)] += DOT(ds, q_l, NN)
            dva_s[part(c)] += DOT(p.astype(jnp.bfloat16), d_l, NN)
            return unused

        def grads_b(j, unused):
            f = flag_of(j)
            q_j, d_j = q_s[g, 1 - f], d_s[g, 1 - f]
            p = sc_b[block(j)] * choose(f, inv_e, inv_l)
            dp = DOT(k_b[block(j), head:], d_j, NT)
            ds = p * (dp - choose(f, delta_e, delta_l))
            ds_e = ds * f.astype(jnp.float32)
            ds_be[block(j)] = ds_e.astype(jnp.bfloat16)
            ds_bl[block(j)] = (ds - ds_e).astype(jnp.bfloat16)
            dkb_s[block(j)] += DOT(ds.astype(jnp.bfloat16), q_j, NN)
            dvb_s[block(j)] += DOT(p.astype(jnp.bfloat16), d_j, NN)
            return unused

        each(steps, 0, grads_a)
        each(n, 0, grads_b)
        dq_l = (DOT(kt_a[...], ds_a[...], NN) + DOT(kt_b[...], ds_bl[...], NN)) * scale
        dq_e = DOT(kt_b[...], ds_be[...], NN) * scale
        for half, dqt in ((0, dq_e), (1, dq_l)):
            dq = dqt.T.astype(jnp.bfloat16)
            dq_st[g, half * span : (half + 1) * span] = jnp.concatenate(
                [dq[h * span : (h + 1) * span] for h in range(quad)], axis=1
            )

        @pl.when(section > 0)
        def _():
            dq_copy(g).start()

    loop(quads, group)

    def terms(j):
        f = flag_m[j, 0].astype(jnp.float32)
        dk_b, dv_b = dkb_s[block(j)], dvb_s[block(j)]
        dk_e, dv_e = dk_b * f, dv_b * f
        return jnp.concatenate(
            [
                jnp.concatenate([(dka_s[block(j)] + dk_e) * scale, dva_s[block(j)] + dv_e], axis=1),
                jnp.concatenate([(dk_b - dk_e) * scale, dv_b - dv_e], axis=1),
            ],
            axis=0,
        )

    def rs_copy(to, slot):
        return pltpu.make_async_remote_copy(
            rs_st.at[to], rs_in.at[slot], rs_send.at[to], rs_recv.at[slot],
            device_id={"ctx": to}, device_id_type=MESH,
        )

    def scatter(i):
        to = peer(i)
        rs_st[to] = terms(to).astype(jnp.bfloat16)
        rs_copy(to, me).start()

    loop(n - 1, scatter)

    def gather(i, acc):
        frm = peer(i)
        rs_copy(frm, frm).wait_recv()
        return acc + rs_in[frm].astype(jnp.float32)

    last = pl.ds(n * span, span)
    diag = jnp.concatenate([dka_s[last] * scale, dva_s[last]], axis=1)
    own = terms(me) + jnp.concatenate([jnp.zeros_like(diag), diag], axis=0)
    kv_st[...] = lax.fori_loop(0, n - 1, gather, own).astype(jnp.bfloat16)
    kvo = pltpu.make_async_remote_copy(
        kv_st, dkv_out.at[0], kvo_send, kvo_recv,
        device_id={"section": section - 1}, device_id_type=MESH,
    )

    @pl.when(section > 0)
    def _():
        kvo.start()

    def drain(i):
        for c in ag_copies(peer(i), me):
            c.wait_send()
        rs_copy(peer(i), me).wait_send()

    loop(n - 1, drain)

    @pl.when(section > 0)
    def _():
        loop(quads, lambda g: dq_copy(g).wait_send())
        kvo.wait_send()

    @pl.when(section < sections - 1)
    def _():
        loop(quads, lambda g: dq_copy(g).wait_recv())
        kvo.wait_recv()


def per_device(sections, n, queries, keys_values, output, dout, segment_ids, span_order):
    head = keys_values.shape[2] // 2
    tok, width = queries.shape[1:]
    heads = width // head
    quads = heads // 4
    span = tok // 2
    wide = 4 * span
    cols = 2 * head
    in_a, in_b = (n + 1) * span, n * span
    any_spec = pl.BlockSpec(memory_space=pl.ANY)
    hbm_spec = pl.BlockSpec(memory_space=pltpu.HBM)
    f32, bf16, i32 = jnp.float32, jnp.bfloat16, jnp.int32
    dma = pltpu.SemaphoreType.DMA
    dq, dkv = pl.pallas_call(
        functools.partial(kernel, sections, n, head, heads),
        out_shape=(
            jax.ShapeDtypeStruct((1, tok, width), bf16),
            jax.ShapeDtypeStruct((1, tok, cols), bf16),
        ),
        in_specs=[hbm_spec] * 5 + [pl.BlockSpec(memory_space=pltpu.SMEM)],
        out_specs=(any_spec, any_spec),
        scratch_shapes=[
            pltpu.VMEM((quads, 2, wide, head), bf16),
            pltpu.VMEM((quads, 2, wide, head), bf16),
            pltpu.VMEM((quads, 2, wide, head), bf16),
            pltpu.VMEM((n, tok, cols), bf16),
            pltpu.VMEM((1, tok), i32),
            pltpu.VMEM((8, tok), i32),
            pltpu.VMEM((n, 8, tok), i32),
            pltpu.VMEM((n, tok), i32),
            pltpu.SMEM((n, tok), i32),
            pltpu.VMEM((in_a, cols), bf16),
            pltpu.VMEM((in_b, cols), bf16),
            pltpu.VMEM((head, in_a + span), bf16),
            pltpu.VMEM((head, in_b), bf16),
            pltpu.VMEM((in_a, tok), f32),
            pltpu.VMEM((in_b, tok), f32),
            pltpu.VMEM((in_a, wide), f32),
            pltpu.VMEM((in_b, wide), f32),
            pltpu.VMEM((in_a + span, wide), bf16),
            pltpu.VMEM((in_b, wide), bf16),
            pltpu.VMEM((in_b, wide), bf16),
            pltpu.VMEM((in_a, head), f32),
            pltpu.VMEM((in_a, head), f32),
            pltpu.VMEM((in_b, head), f32),
            pltpu.VMEM((in_b, head), f32),
            pltpu.VMEM((quads, tok, 4 * head), bf16),
            pltpu.VMEM((n, tok, cols), bf16),
            pltpu.VMEM((n, tok, cols), bf16),
            pltpu.VMEM((tok, cols), bf16),
            dma((3, 2 * heads)),
            dma,
            dma,
            dma,
            dma((2, n)),
            dma((2, n)),
            dma((n,)),
            dma((n,)),
            dma((quads,)),
            dma((quads,)),
            dma,
            dma,
        ],
        compiler_params=pltpu.CompilerParams(
            collective_id=0, has_side_effects=True, vmem_limit_bytes=60 << 20
        ),
    )(queries, keys_values, output, dout, segment_ids, span_order)
    last = lax.axis_index("section") == sections - 1
    return (
        jnp.where(last, jnp.zeros_like(dq), dq),
        jnp.where(last, jnp.zeros_like(dkv), dkv),
    )


def solution(mesh):
    rows = P("section", "ctx", None)
    return jax.shard_map(
        functools.partial(per_device, mesh.shape["section"], mesh.shape["ctx"]),
        mesh=mesh,
        in_specs=(rows, rows, rows, rows, P("section", "ctx"), P("ctx")),
        out_specs=(rows, rows),
        check_vma=False,
    )
```

time: 47.5 us -> 38.2 us (0.80)
  Pallas kernels: 40.4 us -> 34.8 us
  local copies, waits for them, and re-layouts: 4.62 us -> 0.01 us
  other arithmetic: 1.47 us -> 2.55 us
    pallas_call x1, Pallas kernels: 40.4 us -> 34.8 us  [per_device(): pl.pallas_call(functools.partial(kernel, sections, n, head, heads), out_s...]
    unnamed x12 -> x2, local copies, waits for them, and re-layouts: 4.62 us -> 0.01 us
    select_n x1, other arithmetic: 0.83 us -> 1.91 us  [per_device(): jnp.where(last, jnp.zeros_like(dq), dq)]
where the time goes in v2:
time: 38.2 us; the launch traced here: 38.1 us
  Pallas kernels  34.8 us (91%)
  other arithmetic  2.55 us (7%)
  between operations  0.65 us (2%)
    pallas_call x1, Pallas kernels, per_device(): pl.pallas_call(functools.partial(kernel, sections, n, head, heads), out_s...  34.8 us
    select_n x1, other arithmetic, per_device(): jnp.where(last, jnp.zeros_like(dq), dq)  1.91 us

profile of v2, /device:TPU:0, one launch (start us, length us, event | category | flops | bytes accessed | tf_op | source)
XLA Modules:
  0.0 38.1 jit_solution(13287015477746726292)
XLA Ops:
  0.6 34.8 %shard_map.77 = (bf16[1,128,2048]{2,1,0:T(8,128)(2,1)}, bf16[1,128,256]{2,1,0:T(8,128)(2,1)}) custom-call(bf16[1,128,2048]{2,1,0:T(8,128)(2,1)} %q_in.1, bf16[1,128,256]{2,1,0:T(8,128)(2,1)} %kv_in.1, bf16[1,128,2048]{2,1,0:T(8,128)(2,1)} %o_in.1, bf16[1,128,2048]{2,1,0:T(8,128)(2,1)} %d_in.1, s32[1,128]{1,0:T(1,128)} %seg_in.1, s32[2]{0:T(128)} %order_in.1), custom_call_target="tpu_custom_call" | custom-call | tf_op jit(solution)/shard_map/pallas_call | solution.py:347
  35.5 0.0 copy-start
  35.5 1.9 %broadcast_select_fusion = bf16[1,128,2048]{2,1,0:T(8,128)(2,1)} fusion(bf16[1,128,2048]{2,1,0:T(8,128)(2,1)} %get-tuple-element.4, pred[]{:T(512)S(6)} %eq.3), kind=kLoop, calls=%fused_computation | loop fusion | flops 262144 | bytes 1048577 | tf_op jit(solution)/shard_map/jit(_where)/select_n | solution.py:403
  37.4 0.0 copy-done
  37.4 0.6 %broadcast_select_fusion.1 = bf16[1,128,256]{2,1,0:T(8,128)(2,1)} fusion(bf16[1,128,256]{2,1,0:T(8,128)(2,1)S(1)} %copy-done, pred[]{:T(512)S(6)} %eq.3), kind=kLoop, calls=%fused_computation.1 | loop fusion | flops 32768 | bytes 131073 | tf_op jit(solution)/shard_map/jit(_where)/select_n | solution.py:404
Async XLA Ops:
  35.5 1.9 %copy-start = (bf16[1,128,256]{2,1,0:T(8,128)(2,1)S(1)}, bf16[1,128,256]{2,1,0:T(8,128)(2,1)}, u32[]{:S(2)}) copy-start(bf16[1,128,256]{2,1,0:T(8,128)(2,1)} %get-tuple-element.5) | copy-start | bytes 196612

commit v3 on v2

--- a/solution.py
+++ b/solution.py
@@ -19,8 +19,8 @@
     q_in, kv_in, o_in, d_in, seg_in, order_in,
     dq_out, dkv_out,
     q_s, o_s, d_s, kv_s, seg_s, meta_own, meta_s, flag_v, flag_m, k_a, k_b, kt_a, kt_b, bias_a, bias_b,
-    sc_a, sc_b, ds_a, ds_be, ds_bl, dka_s, dva_s, dkb_s, dvb_s, dq_st, rs_st, rs_in, kv_st,
-    in_sem, own_sem, seg_sem, flag_sem, ag_send, ag_recv, rs_send, rs_recv, dq_send, dq_recv, kvo_send, kvo_recv,
+    sc_a, sc_b, ds_a, ds_be, ds_bl, dka_s, dva_s, dkb_s, dvb_s, dq_st, rs_st, rs_mid, rs_in, rs_own, kv_st,
+    in_sem, own_sem, seg_sem, flag_sem, ag_send, ag_recv, rs_send, mid_recv, rs_recv, dq_send, dq_recv, kvo_send, kvo_recv,
 ):
     section = lax.axis_index("section")
     me = lax.axis_index("ctx")
@@ -32,8 +32,15 @@
     def loop(count, body):
         lax.fori_loop(0, count, lambda i, c: (body(i), c)[1], 0)
 
-    def peer(i):
-        return lax.rem(me + i + 1, n)
+    chips = n // 2
+    chip, core = me // 2, lax.rem(me, 2)
+    partner = me + 1 - 2 * core
+
+    def same(i):
+        return 2 * lax.rem(chip + i + 1, chips) + core
+
+    def other(i):
+        return 2 * lax.rem(chip + i + 1, chips) + 1 - core
 
     quad = 4
     quads = heads // quad
@@ -56,10 +63,11 @@
 
     barrier = pltpu.get_barrier_semaphore()
 
-    def greet(i):
-        pl.semaphore_signal(barrier, inc=1, device_id={"ctx": peer(i)}, device_id_type=MESH)
-
-    loop(n - 1, greet)
+    def greet(to):
+        pl.semaphore_signal(barrier, inc=1, device_id={"ctx": to}, device_id_type=MESH)
+
+    loop(chips - 1, lambda i: greet(same(i)))
+    greet(partner)
 
     @pl.when(section > 0)
     def _():
@@ -79,18 +87,33 @@
     meta_own[...] = meta
 
     ends = (section == 0).astype(jnp.int32) + (section == sections - 1).astype(jnp.int32)
-    pl.semaphore_wait(barrier, n + 1 - ends)
-
-    def ag_copies(to, slot):
+    pl.semaphore_wait(barrier, chips + 2 - ends)
+
+    def ag_copies(to, slot, kv, info, via):
         return [
             pltpu.make_async_remote_copy(
-                src, dst.at[slot], ag_send.at[k, to], ag_recv.at[k, slot],
+                src, dst.at[slot], ag_send.at[k, via], ag_recv.at[k, slot],
                 device_id={"ctx": to}, device_id_type=MESH,
             )
-            for k, (src, dst) in enumerate(((kv_in.at[0], kv_s), (meta_own, meta_s)))
+            for k, (src, dst) in enumerate(((info, meta_s), (kv, kv_s)))
         ]
 
-    loop(n - 1, lambda i: [c.start() for c in ag_copies(peer(i), me)][0])
+    def ag_own(to):
+        return ag_copies(to, me, kv_in.at[0], meta_own, to)
+
+    def ag_relay(i):
+        return ag_copies(partner, same(i), kv_s.at[same(i)], meta_s.at[same(i)], other(i))
+
+    def start(copies):
+        for c in copies:
+            c.start()
+
+    def arrived(frm):
+        for c in ag_copies(partner, frm, kv_s.at[frm], meta_s.at[frm], frm):
+            c.wait_recv()
+
+    loop(chips - 1, lambda i: start(ag_own(same(i))))
+    start(ag_own(partner))
 
     meta_s[me] = meta
     for acc in (dka_s, dva_s, dkb_s, dvb_s):
@@ -139,12 +162,21 @@
     own_kv.wait()
     prepare(me)
 
+    arrived(partner)
+    prepare(partner)
+
+    def relay(i):
+        arrived(same(i))
+        start(ag_relay(i))
+        prepare(same(i))
+
+    loop(chips - 1, relay)
+
     def arrive(i):
-        for c in ag_copies(peer(i), peer(i)):
-            c.wait_recv()
-        prepare(peer(i))
-
-    loop(n - 1, arrive)
+        arrived(other(i))
+        prepare(other(i))
+
+    loop(chips - 1, arrive)
     flags = pltpu.make_async_copy(flag_v, flag_m, flag_sem)
     flags.start()
 
@@ -154,7 +186,7 @@
         kt_a[:, at] = k_a[rows, :head].astype(jnp.float32).T.astype(jnp.bfloat16)
         kt_b[:, at] = k_b[rows, :head].astype(jnp.float32).T.astype(jnp.bfloat16)
 
-    loop(n // 2, turn)
+    lax.fori_loop(0, n // 2, lambda j, c: (turn(j), c)[1], 0, unroll=n <= 8)
     kt_a[:, pl.ds(n * span, tok)] = jnp.concatenate(
         [k_a[pl.ds(n * span, span), :head].astype(jnp.float32).T, jnp.zeros((head, span), jnp.float32)],
         axis=1,
@@ -282,28 +314,46 @@
             axis=0,
         )
 
+    def mid_copy(q):
+        return pltpu.make_async_remote_copy(
+            rs_st.at[2 * q + 1 - core], rs_mid.at[q], rs_send.at[2 * q + 1 - core], mid_recv.at[q],
+            device_id={"ctx": partner}, device_id_type=MESH,
+        )
+
     def rs_copy(to, slot):
         return pltpu.make_async_remote_copy(
             rs_st.at[to], rs_in.at[slot], rs_send.at[to], rs_recv.at[slot],
             device_id={"ctx": to}, device_id_type=MESH,
         )
 
+    def hand(i):
+        q = lax.rem(chip + i + 1, chips)
+        rs_st[2 * q + 1 - core] = terms(2 * q + 1 - core).astype(jnp.bfloat16)
+        mid_copy(q).start()
+
+    loop(chips, hand)
+
     def scatter(i):
-        to = peer(i)
-        rs_st[to] = terms(to).astype(jnp.bfloat16)
-        rs_copy(to, me).start()
-
-    loop(n - 1, scatter)
-
-    def gather(i, acc):
-        frm = peer(i)
-        rs_copy(frm, frm).wait_recv()
-        return acc + rs_in[frm].astype(jnp.float32)
+        to = same(i)
+        mid_copy(to // 2).wait_recv()
+        rs_st[to] = (terms(to) + rs_mid[to // 2].astype(jnp.float32)).astype(jnp.bfloat16)
+        rs_copy(to, chip).start()
+
+    loop(chips - 1, scatter)
 
     last = pl.ds(n * span, span)
     diag = jnp.concatenate([dka_s[last] * scale, dva_s[last]], axis=1)
+    mid_copy(chip).wait_recv()
     own = terms(me) + jnp.concatenate([jnp.zeros_like(diag), diag], axis=0)
-    kv_st[...] = lax.fori_loop(0, n - 1, gather, own).astype(jnp.bfloat16)
+    rs_own[...] = own + rs_mid[chip].astype(jnp.float32)
+
+    def gather(i):
+        q = lax.rem(chip + i + 1, chips)
+        rs_copy(same(i), q).wait_recv()
+        rs_own[...] += rs_in[q].astype(jnp.float32)
+
+    loop(chips - 1, gather)
+    kv_st[...] = rs_own[...].astype(jnp.bfloat16)
     kvo = pltpu.make_async_remote_copy(
         kv_st, dkv_out.at[0], kvo_send, kvo_recv,
         device_id={"section": section - 1}, device_id_type=MESH,
@@ -313,12 +363,18 @@
     def _():
         kvo.start()
 
+    def sent(copies):
+        for c in copies:
+            c.wait_send()
+
     def drain(i):
-        for c in ag_copies(peer(i), me):
-            c.wait_send()
-        rs_copy(peer(i), me).wait_send()
-
-    loop(n - 1, drain)
+        sent(ag_own(same(i)))
+        sent(ag_relay(i))
+        rs_copy(same(i), chip).wait_send()
+
+    loop(chips - 1, drain)
+    sent(ag_own(partner))
+    loop(chips, lambda q: mid_copy(q).wait_send())
 
     @pl.when(section > 0)
     def _():
@@ -379,7 +435,9 @@
             pltpu.VMEM((in_b, head), f32),
             pltpu.VMEM((quads, tok, 4 * head), bf16),
             pltpu.VMEM((n, tok, cols), bf16),
-            pltpu.VMEM((n, tok, cols), bf16),
+            pltpu.VMEM((n // 2, tok, cols), bf16),
+            pltpu.VMEM((n // 2, tok, cols), bf16),
+            pltpu.VMEM((tok, cols), f32),
             pltpu.VMEM((tok, cols), bf16),
             dma((3, 2 * heads)),
             dma,
@@ -388,16 +446,23 @@
             dma((2, n)),
             dma((2, n)),
             dma((n,)),
-            dma((n,)),
+            dma((n // 2,)),
+            dma((n // 2,)),
             dma((quads,)),
             dma((quads,)),
             dma,
             dma,
         ],
         compiler_params=pltpu.CompilerParams(
-            collective_id=0, has_side_effects=True, vmem_limit_bytes=60 << 20
+            collective_id=0, has_side_effects=True, vmem_limit_bytes=(32 << 20) + n * (448 << 10)
         ),
-    )(queries, keys_values, output, dout, segment_ids, span_order)
+    )(
+        *[
+            pltpu.with_memory_space_constraint(x, pltpu.HBM)
+            for x in (queries, keys_values, output, dout, segment_ids)
+        ],
+        span_order,
+    )
     last = lax.axis_index("section") == sections - 1
     return (
         jnp.where(last, jnp.zeros_like(dq), dq),

time: 38.2 us -> 33.4 us (0.87)
  Pallas kernels: 34.8 us -> 30.5 us
  other arithmetic: 2.55 us -> 1.47 us
  local copies, waits for them, and re-layouts: 0.01 us -> 0.65 us
    pallas_call x1, Pallas kernels: 34.8 us -> 30.5 us  [per_device(): pl.pallas_call(functools.partial(kernel, sections, n, head, heads), out_s...]
    select_n x1, other arithmetic: 1.91 us -> 0.83 us  [per_device(): jnp.where(last, jnp.zeros_like(dq), dq)]
    unnamed x2, local copies, waits for them, and re-layouts: 0.01 us -> 0.65 us
where the time goes in v3:
time: 33.4 us; the launch traced here: 33.2 us
  Pallas kernels  30.5 us (91%)
  other arithmetic  1.47 us (4%)
  local copies, waits for them, and re-layouts  0.65 us (2%)
  between operations  0.65 us (2%)
    pallas_call x1, Pallas kernels, per_device(): pl.pallas_call(functools.partial(kernel, sections, n, head, heads), out_s...  30.5 us
    select_n x1, other arithmetic, per_device(): jnp.where(last, jnp.zeros_like(dq), dq)  0.83 us

profile of v3, /device:TPU:0, one launch (start us, length us, event | category | flops | bytes accessed | tf_op | source)
XLA Modules:
  0.0 33.2 jit_solution(1260555414384044220)
XLA Ops:
  0.6 0.0 copy-start
  0.6 0.6 %copy-done = s32[2]{0:T(128)S(1)} copy-done((s32[2]{0:T(128)S(1)}, s32[2]{0:T(128)}, u32[]{:S(2)}) %copy-start) | copy-done | bytes 32
  1.3 30.5 %shard_map.77 = (bf16[1,128,2048]{2,1,0:T(8,128)(2,1)S(1)}, bf16[1,128,256]{2,1,0:T(8,128)(2,1)S(1)}) custom-call(bf16[1,128,2048]{2,1,0:T(8,128)(2,1)} %q_in.1, bf16[1,128,256]{2,1,0:T(8,128)(2,1)} %kv_in.1, bf16[1,128,2048]{2,1,0:T(8,128)(2,1)} %o_in.1, bf16[1,128,2048]{2,1,0:T(8,128)(2,1)} %d_in.1, s32[1,128]{1,0:T(1,128)} %seg_in.1, s32[2]{0:T(128)S(1)} %copy-done), custom_call_target="tpu_custom_call" | custom-call | tf_op jit(solution)/shard_map/pallas_call | solution.py:403
  31.8 0.8 %broadcast_select_fusion = bf16[1,128,2048]{2,1,0:T(8,128)(2,1)} fusion(bf16[1,128,2048]{2,1,0:T(8,128)(2,1)S(1)} %get-tuple-element.4, pred[]{:T(512)S(6)} %eq.3), kind=kLoop, calls=%fused_computation | loop fusion | flops 262144 | bytes 1048577 | tf_op jit(solution)/shard_map/jit(_where)/select_n | solution.py:468
  32.6 0.6 %broadcast_select_fusion.1 = bf16[1,128,256]{2,1,0:T(8,128)(2,1)} fusion(bf16[1,128,256]{2,1,0:T(8,128)(2,1)S(1)} %get-tuple-element.5, pred[]{:T(512)S(6)} %eq.3), kind=kLoop, calls=%fused_computation.1 | loop fusion | flops 32768 | bytes 131073 | tf_op jit(solution)/shard_map/jit(_where)/select_n | solution.py:469
Async XLA Ops:
  0.6 0.7 %copy-start = (s32[2]{0:T(128)S(1)}, s32[2]{0:T(128)}, u32[]{:S(2)}) copy-start(s32[2]{0:T(128)} %order_in.1) | copy-start | bytes 28

commit v4 on v3

--- a/solution.py
+++ b/solution.py
@@ -18,8 +18,8 @@
     sections, n, head, heads,
     q_in, kv_in, o_in, d_in, seg_in, order_in,
     dq_out, dkv_out,
-    q_s, o_s, d_s, kv_s, seg_s, meta_own, meta_s, flag_v, flag_m, k_a, k_b, kt_a, kt_b, bias_a, bias_b,
-    sc_a, sc_b, ds_a, ds_be, ds_bl, dka_s, dva_s, dkb_s, dvb_s, dq_st, rs_st, rs_mid, rs_in, rs_own, kv_st,
+    q_s, o_s, d_s, kv_s, seg_s, meta_own, meta_s, flag_m, k_a, k_b, kt_a, kt_b, bias_a, bias_b,
+    sc_a, sc_b, ds_a, p_a, ds_b, p_b, ds_be, ds_bl, dka_s, dva_s, dkb_s, dvb_s, dq_st, rs_st, rs_mid, rs_in, rs_own, kv_st,
     in_sem, own_sem, seg_sem, flag_sem, ag_send, ag_recv, rs_send, mid_recv, rs_recv, dq_send, dq_recv, kvo_send, kvo_recv,
 ):
     section = lax.axis_index("section")
@@ -77,7 +77,6 @@
     def _():
         pl.semaphore_signal(barrier, inc=1, device_id={"section": section + 1}, device_id_type=MESH)
 
-    loop(2 * heads, lambda g: [c.start() for c in in_copies(g)][0])
 
     lane = lax.broadcasted_iota(jnp.int32, (1, tok), 1)
     pos_row = jnp.where(lane < span, order_in[0] * span + lane, order_in[1] * span + lane - span)
@@ -114,6 +113,7 @@
 
     loop(chips - 1, lambda i: start(ag_own(same(i))))
     start(ag_own(partner))
+    loop(2 * heads, lambda i: start(in_copies(i)))
 
     meta_s[me] = meta
     for acc in (dka_s, dva_s, dkb_s, dvb_s):
@@ -136,12 +136,15 @@
     def block(j):
         return pl.ds(pl.multiple_of(j * span, span), span)
 
+    def flag_copy(j):
+        return pltpu.make_async_copy(meta_s.at[j], flag_m.at[j], flag_sem.at[j])
+
     def prepare(j):
+        flag_copy(j).start()
         got = meta_s[j]
         info = got.astype(jnp.float32).T
         kv = kv_s[j].astype(jnp.float32)
         flag = got[2:3] <= order_in[0]
-        flag_v[pl.ds(j, 1)] = flag.astype(jnp.int32)
         bias_a[block(j)] = bias_of(info[:span], pos_l, seg_l)
         k_a[block(j)] = kv_s[j, :span]
         kind = jnp.where(flag, 1.0, 0.0)
@@ -159,40 +162,40 @@
             k_a[last] = kv_s[j, span:]
             bias_a[last] = bias_of(info[span:], pos_l, seg_l)
 
-    own_kv.wait()
-    prepare(me)
-
-    arrived(partner)
-    prepare(partner)
-
-    def relay(i):
-        arrived(same(i))
-        start(ag_relay(i))
-        prepare(same(i))
-
-    loop(chips - 1, relay)
-
-    def arrive(i):
-        arrived(other(i))
-        prepare(other(i))
-
-    loop(chips - 1, arrive)
-    flags = pltpu.make_async_copy(flag_v, flag_m, flag_sem)
-    flags.start()
-
     def turn(j):
         at = pl.ds(pl.multiple_of(j * tok, tok), tok)
         rows = pl.ds(pl.multiple_of(j * tok, tok), tok)
         kt_a[:, at] = k_a[rows, :head].astype(jnp.float32).T.astype(jnp.bfloat16)
         kt_b[:, at] = k_b[rows, :head].astype(jnp.float32).T.astype(jnp.bfloat16)
 
-    lax.fori_loop(0, n // 2, lambda j, c: (turn(j), c)[1], 0, unroll=n <= 8)
+    own_kv.wait()
+    prepare(me)
+
     kt_a[:, pl.ds(n * span, tok)] = jnp.concatenate(
         [k_a[pl.ds(n * span, span), :head].astype(jnp.float32).T, jnp.zeros((head, span), jnp.float32)],
         axis=1,
     ).astype(jnp.bfloat16)
-    loop(2 * heads, lambda g: [c.wait() for c in in_copies(g)][0])
-    flags.wait()
+    arrived(partner)
+    prepare(partner)
+    turn(chip)
+
+    def relay(i):
+        arrived(same(i))
+        start(ag_relay(i))
+        prepare(same(i))
+
+    loop(chips - 1, relay)
+
+    loop(2 * heads, lambda i: [c.wait() for c in in_copies(i)][0])
+
+    def arrive(i):
+        arrived(other(i))
+        prepare(other(i))
+        turn(other(i) // 2)
+
+    loop(chips - 1, arrive)
+
+    loop(n, lambda j: flag_copy(j).wait())
 
     def dq_copy(g):
         at = pl.ds(pl.multiple_of(g * quad * head, quad * head), quad * head)
@@ -224,7 +227,7 @@
         delta_e, delta_l = delta_of(0), delta_of(1)
 
         def flag_of(j):
-            return flag_m[j, 0]
+            return (flag_m[j, 2, 0] <= order_in[0]).astype(jnp.int32)
 
         def choose(f, early, late):
             return jnp.where(f > 0, early, late)
@@ -269,21 +272,19 @@
             dp = DOT(k_a[part(c), head:], d_l, NT)
             ds = (p * (dp - delta_l)).astype(jnp.bfloat16)
             ds_a[part(c)] = ds
-            dka_s[part(c)] += DOT(ds, q_l, NN)
-            dva_s[part(c)] += DOT(p.astype(jnp.bfloat16), d_l, NN)
+            p_a[part(c)] = p.astype(jnp.bfloat16)
             return unused
 
         def grads_b(j, unused):
             f = flag_of(j)
-            q_j, d_j = q_s[g, 1 - f], d_s[g, 1 - f]
             p = sc_b[block(j)] * choose(f, inv_e, inv_l)
-            dp = DOT(k_b[block(j), head:], d_j, NT)
+            dp = DOT(k_b[block(j), head:], d_s[g, 1 - f], NT)
             ds = p * (dp - choose(f, delta_e, delta_l))
             ds_e = ds * f.astype(jnp.float32)
             ds_be[block(j)] = ds_e.astype(jnp.bfloat16)
             ds_bl[block(j)] = (ds - ds_e).astype(jnp.bfloat16)
-            dkb_s[block(j)] += DOT(ds.astype(jnp.bfloat16), q_j, NN)
-            dvb_s[block(j)] += DOT(p.astype(jnp.bfloat16), d_j, NN)
+            ds_b[block(j)] = ds.astype(jnp.bfloat16)
+            p_b[block(j)] = p.astype(jnp.bfloat16)
             return unused
 
         each(steps, 0, grads_a)
@@ -300,10 +301,24 @@
         def _():
             dq_copy(g).start()
 
+        def terms_a(c, unused):
+            dka_s[part(c)] += DOT(ds_a[part(c)], q_l, NN)
+            dva_s[part(c)] += DOT(p_a[part(c)], d_l, NN)
+            return unused
+
+        def terms_b(j, unused):
+            f = flag_of(j)
+            dkb_s[block(j)] += DOT(ds_b[block(j)], q_s[g, 1 - f], NN)
+            dvb_s[block(j)] += DOT(p_b[block(j)], d_s[g, 1 - f], NN)
+            return unused
+
+        each(steps, 0, terms_a)
+        each(n, 0, terms_b)
+
     loop(quads, group)
 
     def terms(j):
-        f = flag_m[j, 0].astype(jnp.float32)
+        f = (flag_m[j, 2, 0] <= order_in[0]).astype(jnp.float32)
         dk_b, dv_b = dkb_s[block(j)], dvb_s[block(j)]
         dk_e, dv_e = dk_b * f, dv_b * f
         return jnp.concatenate(
@@ -416,8 +431,7 @@
             pltpu.VMEM((1, tok), i32),
             pltpu.VMEM((8, tok), i32),
             pltpu.VMEM((n, 8, tok), i32),
-            pltpu.VMEM((n, tok), i32),
-            pltpu.SMEM((n, tok), i32),
+            pltpu.SMEM((n, 8, tok), i32),
             pltpu.VMEM((in_a, cols), bf16),
             pltpu.VMEM((in_b, cols), bf16),
             pltpu.VMEM((head, in_a + span), bf16),
@@ -427,6 +441,9 @@
             pltpu.VMEM((in_a, wide), f32),
             pltpu.VMEM((in_b, wide), f32),
             pltpu.VMEM((in_a + span, wide), bf16),
+            pltpu.VMEM((in_a, wide), bf16),
+            pltpu.VMEM((in_b, wide), bf16),
+            pltpu.VMEM((in_b, wide), bf16),
             pltpu.VMEM((in_b, wide), bf16),
             pltpu.VMEM((in_b, wide), bf16),
             pltpu.VMEM((in_a, head), f32),
@@ -442,7 +459,7 @@
             dma((3, 2 * heads)),
             dma,
             dma,
-            dma,
+            dma((n,)),
             dma((2, n)),
             dma((2, n)),
             dma((n,)),

time: 33.4 us -> 32.9 us (0.985)
  Pallas kernels: 30.5 us -> 29.9 us
    pallas_call x1, Pallas kernels: 30.5 us -> 29.9 us  [per_device(): pl.pallas_call(functools.partial(kernel, sections, n, head, heads), out_s...]
where the time goes in v4:
time: 32.9 us; the launch traced here: 32.7 us
  Pallas kernels  29.9 us (91%)
  other arithmetic  1.47 us (4%)
  local copies, waits for them, and re-layouts  0.65 us (2%)
  between operations  0.65 us (2%)
    pallas_call x1, Pallas kernels, per_device(): pl.pallas_call(functools.partial(kernel, sections, n, head, heads), out_s...  29.9 us
    select_n x1, other arithmetic, per_device(): jnp.where(last, jnp.zeros_like(dq), dq)  0.83 us

profile of v4, /device:TPU:0, one launch (start us, length us, event | category | flops | bytes accessed | tf_op | source)
XLA Modules:
  0.0 32.7 jit_solution(896044640942706125)
XLA Ops:
  0.6 0.0 copy-start
  0.6 0.6 %copy-done = s32[2]{0:T(128)S(1)} copy-done((s32[2]{0:T(128)S(1)}, s32[2]{0:T(128)}, u32[]{:S(2)}) %copy-start) | copy-done | bytes 32
  1.3 29.9 %shard_map.77 = (bf16[1,128,2048]{2,1,0:T(8,128)(2,1)S(1)}, bf16[1,128,256]{2,1,0:T(8,128)(2,1)S(1)}) custom-call(bf16[1,128,2048]{2,1,0:T(8,128)(2,1)} %q_in.1, bf16[1,128,256]{2,1,0:T(8,128)(2,1)} %kv_in.1, bf16[1,128,2048]{2,1,0:T(8,128)(2,1)} %o_in.1, bf16[1,128,2048]{2,1,0:T(8,128)(2,1)} %d_in.1, s32[1,128]{1,0:T(1,128)} %seg_in.1, s32[2]{0:T(128)S(1)} %copy-done), custom_call_target="tpu_custom_call" | custom-call | tf_op jit(solution)/shard_map/pallas_call | solution.py:418
  31.2 0.8 %broadcast_select_fusion = bf16[1,128,2048]{2,1,0:T(8,128)(2,1)} fusion(bf16[1,128,2048]{2,1,0:T(8,128)(2,1)S(1)} %get-tuple-element.4, pred[]{:T(512)S(6)} %eq.3), kind=kLoop, calls=%fused_computation | loop fusion | flops 262144 | bytes 1048577 | tf_op jit(solution)/shard_map/jit(_where)/select_n | solution.py:485
  32.1 0.6 %broadcast_select_fusion.1 = bf16[1,128,256]{2,1,0:T(8,128)(2,1)} fusion(bf16[1,128,256]{2,1,0:T(8,128)(2,1)S(1)} %get-tuple-element.5, pred[]{:T(512)S(6)} %eq.3), kind=kLoop, calls=%fused_computation.1 | loop fusion | flops 32768 | bytes 131073 | tf_op jit(solution)/shard_map/jit(_where)/select_n | solution.py:486
Async XLA Ops:
  0.6 0.7 %copy-start = (s32[2]{0:T(128)S(1)}, s32[2]{0:T(128)}, u32[]{:S(2)}) copy-start(s32[2]{0:T(128)} %order_in.1) | copy-start | bytes 28

commit v5 on v4

--- a/solution.py
+++ b/solution.py
@@ -30,7 +30,7 @@
     scale = head ** (-0.5)
 
     def loop(count, body):
-        lax.fori_loop(0, count, lambda i, c: (body(i), c)[1], 0)
+        lax.fori_loop(0, count, lambda i, c: (body(i), c)[1], 0, unroll=count <= 4)
 
     chips = n // 2
     chip, core = me // 2, lax.rem(me, 2)

time: 32.9 us -> 32.2 us (0.979)
  Pallas kernels: 29.9 us -> 29.2 us
    pallas_call x1, Pallas kernels: 29.9 us -> 29.2 us  [per_device(): pl.pallas_call(functools.partial(kernel, sections, n, head, heads), out_s...]
where the time goes in v5:
time: 32.2 us; the launch traced here: 32 us
  Pallas kernels  29.2 us (91%)
  other arithmetic  1.47 us (5%)
  local copies, waits for them, and re-layouts  0.65 us (2%)
  between operations  0.65 us (2%)
    pallas_call x1, Pallas kernels, per_device(): pl.pallas_call(functools.partial(kernel, sections, n, head, heads), out_s...  29.2 us
    select_n x1, other arithmetic, per_device(): jnp.where(last, jnp.zeros_like(dq), dq)  0.83 us
    unnamed x2, local copies, waits for them, and re-layouts  0.65 us

profile of v5, /device:TPU:0, one launch (start us, length us, event | category | flops | bytes accessed | tf_op | source)
XLA Modules:
  0.0 32.0 jit_solution(8087961367403013441)
XLA Ops:
  0.6 0.0 copy-start
  0.6 0.6 %copy-done = s32[2]{0:T(128)S(1)} copy-done((s32[2]{0:T(128)S(1)}, s32[2]{0:T(128)}, u32[]{:S(2)}) %copy-start) | copy-done | bytes 32
  1.3 29.2 %shard_map.77 = (bf16[1,128,2048]{2,1,0:T(8,128)(2,1)S(1)}, bf16[1,128,256]{2,1,0:T(8,128)(2,1)S(1)}) custom-call(bf16[1,128,2048]{2,1,0:T(8,128)(2,1)} %q_in.1, bf16[1,128,256]{2,1,0:T(8,128)(2,1)} %kv_in.1, bf16[1,128,2048]{2,1,0:T(8,128)(2,1)} %o_in.1, bf16[1,128,2048]{2,1,0:T(8,128)(2,1)} %d_in.1, s32[1,128]{1,0:T(1,128)} %seg_in.1, s32[2]{0:T(128)S(1)} %copy-done), custom_call_target="tpu_custom_call" | custom-call | tf_op jit(solution)/shard_map/pallas_call | solution.py:418
  30.5 0.8 %broadcast_select_fusion = bf16[1,128,2048]{2,1,0:T(8,128)(2,1)} fusion(bf16[1,128,2048]{2,1,0:T(8,128)(2,1)S(1)} %get-tuple-element.4, pred[]{:T(512)S(6)} %eq.3), kind=kLoop, calls=%fused_computation | loop fusion | flops 262144 | bytes 1048577 | tf_op jit(solution)/shard_map/jit(_where)/select_n | solution.py:485
  31.4 0.6 %broadcast_select_fusion.1 = bf16[1,128,256]{2,1,0:T(8,128)(2,1)} fusion(bf16[1,128,256]{2,1,0:T(8,128)(2,1)S(1)} %get-tuple-element.5, pred[]{:T(512)S(6)} %eq.3), kind=kLoop, calls=%fused_computation.1 | loop fusion | flops 32768 | bytes 131073 | tf_op jit(solution)/shard_map/jit(_where)/select_n | solution.py:486
Async XLA Ops:
  0.6 0.7 %copy-start = (s32[2]{0:T(128)S(1)}, s32[2]{0:T(128)}, u32[]{:S(2)}) copy-start(s32[2]{0:T(128)} %order_in.1) | copy-start | bytes 28
